TPU v7x, 256 devices: a whole 4x4x8 slice. The times are simulated.
256 devices in a mesh: space: 64 (over x, y, z_lo), load: 4 (over z_hi, core).
Axes of the slice: x: 4, y: 4, z: 8 (z_hi: 2, z_lo: 4; z = z_hi * 4 + z_lo), core: 2. Of those that a mesh axis runs over, the one named last changes fastest.
Arguments:
- load_force: float32 [4, 3, 512, 16, 256], P('load', None, 'space'), may hold values from -6 to 6
- stiffness: float32 [512, 16, 256], P('space'), may hold values from 0.5 to 4
- material: int32 [64, 2], P('space'), may hold values from 0 to 2
- face_src: int32 [64, 64, 256], P('space'), may hold values from 0 to 32767
- face_count: int32 [64, 64], P('space'), may hold values from 0 to 256, as said below
- face_dst: int32 [64, 64, 256], P('space'), may hold values from 0 to 4095
Outputs:
- displacement: float32 [4, 3, 512, 16, 256], P('load', None, 'space')
- sensitivity: float32 [3, 512, 16, 256], P(None, 'space', 'load')
Inputs may be any that keep to these rules, and one draw needn't show every extreme that they name: face_count[s, o] counts the live first slots from slab s to owner o; in every row one owner gets all 256.
All inputs are finite; a program needn't handle non-finite values.
Results may differ from a plain program's by a relative error of at most 0.0001.
Values sent between devices are 32-bit elements; how exact they have to be, the bound alone decides.
No kernel may reach another device: no remote copies, remote signals or barrier semaphores. Data moves between devices by JAX's collectives and lax.ppermute only.
A program may use at most 192 MiB of HBM per device.

v0:
```python
import jax
import jax.numpy as jnp
from jax import lax
from jax.sharding import PartitionSpec as P

NY = 16
BY = 8
SLOTS = 256
FINE_STEPS = 3
COARSE_STEPS = 4
UPPER_EDGE = 2.1
LOWER_EDGE = 0.15
COUPLING = 0.1
MODULI = (1.0, 0.55, 0.25)


def extended(block, sides, width):
    for axis, dim in sides:
        count = lax.axis_size(axis)
        forward = [(i, i + 1) for i in range(count - 1)]
        backward = [(target, source) for source, target in forward]
        low = lax.ppermute(
            lax.slice_in_dim(block, block.shape[dim] - width, None, axis=dim), axis, forward
        )
        high = lax.ppermute(lax.slice_in_dim(block, 0, width, axis=dim), axis, backward)
        block = jnp.concatenate([low, block, high], axis=dim)
    return block


def neighbour_list():
    entries = []
    for shift_x in (-1, 0, 1):
        for shift_y in (-1, 0, 1):
            for shift_z in (-1, 0, 1):
                reach_len = abs(shift_x) + abs(shift_y) + abs(shift_z)
                if reach_len > 0:
                    entries.append(
                        (shift_x, shift_y, shift_z, (1.0, 0.5, 0.25)[reach_len - 1] / 14.0)
                    )
    return entries


def window(padded, shift_x, shift_y, shift_z, inner_shape):
    size_x, size_y, size_z = inner_shape
    return padded[
        :,
        1 + shift_x : 1 + shift_x + size_x,
        1 + shift_y : 1 + shift_y + size_y,
        1 + shift_z : 1 + shift_z + size_z,
    ]


def operate(padded_field, padded_coef):
    inner_shape = (padded_field.shape[1] - 2, padded_field.shape[2] - 2, padded_field.shape[3] - 2)
    centre = window(padded_field, 0, 0, 0, inner_shape)
    coef_mid = window(padded_coef, 0, 0, 0, inner_shape)
    result = jnp.zeros_like(centre)
    for shift_x, shift_y, shift_z, weight in neighbour_list():
        face_coef = 0.5 * (coef_mid + window(padded_coef, shift_x, shift_y, shift_z, inner_shape))
        result = result + weight * face_coef * (
            centre - window(padded_field, shift_x, shift_y, shift_z, inner_shape)
        )
    pieces = []
    for component in range(3):
        mixed_term = jnp.zeros_like(coef_mid[0])
        for partner in range(3):
            if partner != component:
                for sign_a in (1, -1):
                    for sign_b in (1, -1):
                        offset = [0, 0, 0]
                        offset[component] += sign_a
                        offset[partner] += sign_b
                        mixed_term = (
                            mixed_term
                            + 0.25
                            * sign_a
                            * sign_b
                            * window(
                                padded_field[partner : partner + 1],
                                offset[0],
                                offset[1],
                                offset[2],
                                inner_shape,
                            )[0]
                        )
        pieces.append(result[component] - COUPLING * coef_mid[0] * mixed_term)
    return jnp.stack(pieces)


def diagonal_of(padded_coef):
    inner_shape = (padded_coef.shape[1] - 2, padded_coef.shape[2] - 2, padded_coef.shape[3] - 2)
    coef_mid = window(padded_coef, 0, 0, 0, inner_shape)
    total_sum = jnp.zeros_like(coef_mid)
    for shift_x, shift_y, shift_z, weight in neighbour_list():
        total_sum = total_sum + weight * 0.5 * (
            coef_mid + window(padded_coef, shift_x, shift_y, shift_z, inner_shape)
        )
    return total_sum


def pad_sides(grid_field):
    return jnp.pad(grid_field, ((0, 0), (0, 0), (1, 1), (1, 1)))


def chebyshev(source, padded_coef, diagonal, sweep_count, widen):
    midpoint = (UPPER_EDGE + LOWER_EDGE) / 2.0
    halfwidth = (UPPER_EDGE - LOWER_EDGE) / 2.0
    spread_ratio = midpoint / halfwidth
    rho_old = 1.0 / spread_ratio
    update = source / (midpoint * diagonal)
    solution = update
    for sweep_idx in range(1, sweep_count):
        residual = source - operate(widen(solution), padded_coef)
        rho_new = 1.0 / (2.0 * spread_ratio - rho_old)
        update = rho_new * rho_old * update + 2.0 * rho_new / halfwidth * residual / diagonal
        solution = solution + update
        rho_old = rho_new
    return solution


def coarsen(grid_field):
    comps, size_x, size_y, size_z = grid_field.shape
    return grid_field.reshape(comps, size_x // 2, 2, size_y // 2, 2, size_z // 2, 2).mean(
        axis=(2, 4, 6)
    )


def refine(grid_field):
    return jnp.repeat(jnp.repeat(jnp.repeat(grid_field, 2, axis=1), 2, axis=2), 2, axis=3)


def modulus_rows(material, brick_rows):
    onehot = (material[..., None] == jnp.arange(len(MODULI), dtype=jnp.int32)).astype(jnp.float32)
    values = jnp.sum(onehot * jnp.array(MODULI, jnp.float32), axis=-1)
    return jnp.repeat(values, brick_rows, axis=-1)


def widen_fine(grid_field):
    planes = extended(grid_field, (("space", 1),), 1)
    return pad_sides(planes)


def body(load_force, stiffness, material, face_src, face_count, face_dst):
    own_cells = modulus_rows(material, BY)[0][None, :, None]
    coef = stiffness * own_cells
    padded_coef = widen_fine(coef[None])
    diag_fine = diagonal_of(padded_coef)
    coarse_coef = coarsen(coef[None])

    def widen_coarse(grid_field):
        planes = extended(grid_field, (("space", 1),), 1)
        return pad_sides(planes)

    padded_coarse = widen_coarse(coarse_coef)
    diag_coarse = diagonal_of(padded_coarse)
    live_mask = (jnp.arange(SLOTS, dtype=jnp.int32)[None, :] < face_count[0][:, None]).astype(
        jnp.float32
    )
    source = load_force[0]
    smooth = chebyshev(source, padded_coef, diag_fine, FINE_STEPS, widen_fine)
    smooth, residual = (smooth, source - operate(widen_fine(smooth), padded_coef))
    coarse_source = 4.0 * coarsen(residual)
    picked = residual.reshape(3, -1)[:, face_src[0]] * live_mask[None]
    arrived = lax.all_to_all(picked, "space", split_axis=1, concat_axis=1, tiled=True)
    coarse_source = (
        coarse_source.reshape(3, -1).at[:, face_dst[0]].add(arrived).reshape(coarse_source.shape)
    )
    displaced = smooth + refine(
        chebyshev(coarse_source, padded_coarse, diag_coarse, COARSE_STEPS, widen_coarse)
    )
    image = operate(widen_fine(displaced), padded_coef)
    energy = jnp.sum(displaced * image, axis=0)
    outputs = [displaced]
    rows_part = NY // lax.axis_size("load")
    start_row = lax.axis_index("load") * rows_part
    total_sum = lax.psum(energy, "load")
    energy_part = lax.dynamic_slice_in_dim(total_sum, start_row, rows_part, 1)
    own_part = lax.dynamic_slice_in_dim(own_cells, start_row, rows_part, 1)[None]
    moduli = jnp.array(MODULI, jnp.float32)[:, None, None, None]
    sensitivity = (moduli - own_part) / own_part * energy_part[None]
    return (jnp.stack(outputs), sensitivity)


def solution(mesh):
    return jax.shard_map(
        body,
        mesh=mesh,
        in_specs=(
            P("load", None, "space", None, None),
            P("space", None, None),
            P("space", None),
            P("space", None, None),
            P("space", None),
            P("space", None, None),
        ),
        out_specs=(P("load", None, "space", None, None), P(None, "space", "load", None)),
        check_vma=False,
    )
```

profile of v0, /device:TPU:1, one launch (start us, length us, event | category | flops | bytes accessed | tf_op | source)
XLA Modules:
  0.0 533.6 jit_solution(4295424980780647665)
XLA Ops:
  8.2 1.0 fusion.729
  9.2 1.3 collective-permute-start.1
  10.5 5.0 collective-permute-start
  16.5 9.8 %reshape_broadcast_in_dim.3 = f32[4,2,8,2,128,2]{5,4,3,2,1,0:T(8,128)} reshape(f32[8,16,256]{2,1,0:T(8,128)S(1)} %broadcast_multiply_fusion.1) | data formatting | bytes 262144 | tf_op jit(solution)/shard_map/reshape;broadcast_in_dim | solution.py:123
  26.3 4.1 reduce_sum.38
  30.4 1.3 collective-permute-start.9
  31.7 4.2 collective-permute-start.8
  37.3 26.5 %squeeze.11 = f32[3,4,2,8,2,128,2]{6,5,4,3,2,1,0:T(8,128)} reshape(f32[1,3,8,16,256]{4,3,2,1,0:T(8,128)S(1)} %copy-done) | data formatting | bytes 786432 | tf_op jit(solution)/shard_map/squeeze | solution.py:159
  63.9 8.6 %copy.310 = f32[1,3,8,16,256]{1,4,3,2,0:T(8,128)} copy(f32[1,3,8,16,256]{4,3,2,1,0:T(8,128)S(1)} %copy-done) | data formatting | bytes 786432 | tf_op args[0]
  74.9 1.3 collective-permute-start.3
  76.2 4.2 collective-permute-start.2
  81.9 2.0 fusion.164
  84.8 1.3 collective-permute-start.5
  86.1 6.7 %collective-permute-start.4 = (f32[3,1,16,256]{3,2,1,0:T(8,128)S(1)}, f32[3,1,16,256]{3,2,1,0:T(8,128)S(1)}, u32[]{:S(2)}, u32[]{:S(2)}) collective-permute-start(f32[3,1,16,256]{3,2,1,0:T(8,128)S(1)} %get-tuple-element.56), channel_id=1, source_target_pairs={{0,4},{4,8},{8,12},{12,16},{16,20},{20,24},{24,28},{28,32},{32,36}... | collective-permute-start | bytes 147464 | tf_op jit(solution)/shard_map/ppermute | solution.py:22
  94.3 2.0 fusion.111
  97.4 1.3 collective-permute-start.7
  98.7 6.9 %collective-permute-start.6 = (f32[3,1,16,256]{3,2,1,0:T(8,128)S(1)}, f32[3,1,16,256]{3,2,1,0:T(8,128)S(1)}, u32[]{:S(2)}, u32[]{:S(2)}) collective-permute-start(f32[3,1,16,256]{3,2,1,0:T(8,128)S(1)} %get-tuple-element.54), channel_id=1, source_target_pairs={{0,4},{4,8},{8,12},{12,16},{16,20},{20,24},{24,28},{28,32},{32,36}... | collective-permute-start | bytes 147464 | tf_op jit(solution)/shard_map/ppermute | solution.py:22
  107.2 2.0 fusion.58
  109.9 9.7 %stack.91 = f32[1,4,2,8,2,128,2]{6,5,4,3,2,1,0:T(8,128)} reshape(f32[1,8,16,256]{3,2,1,0:T(8,128)S(1)} %fusion.270) | data formatting | bytes 262144 | tf_op jit(solution)/shard_map/stack | solution.py:87
  119.6 9.7 %stack.90 = f32[1,4,2,8,2,128,2]{6,5,4,3,2,1,0:T(8,128)} reshape(f32[1,8,16,256]{3,2,1,0:T(8,128)S(1)} %get-tuple-element.23) | data formatting | bytes 262144 | tf_op jit(solution)/shard_map/stack | solution.py:87
  129.4 9.7 %stack.89 = f32[1,4,2,8,2,128,2]{6,5,4,3,2,1,0:T(8,128)} reshape(f32[1,8,16,256]{3,2,1,0:T(8,128)S(1)} %get-tuple-element.22) | data formatting | bytes 262144 | tf_op jit(solution)/shard_map/stack | solution.py:87
  139.9 8.6 %copy.311 = f32[3,32768]{0,1:T(8,128)} copy(f32[3,32768]{1,0:T(4,128)S(1)} %pad_maximum_fusion) | data formatting | bytes 786432 | tf_op jit(solution)/shard_map/stack | solution.py:87
  148.5 17.8 %bitcast_subtract_fusion = f32[3,32768]{0,1:T(8,128)} fusion(f32[3,32768]{0,1:T(8,128)} %copy.311, f32[1,3,8,16,256]{1,4,3,2,0:T(8,128)} %copy.310), kind=kLoop, calls=%fused_computation.4 | loop fusion | flops 98304 | bytes 1179648 | tf_op jit(solution)/shard_map/sub | solution.py:161
  166.3 60.5 %gather_fusion = f32[16384,3]{1,0:T(8,128)} fusion(f32[3,32768]{0,1:T(8,128)} %bitcast_subtract_fusion, s32[16384]{0:T(1024)S(1)} %copy-done.77), kind=kCustom, calls=%fused_computation | custom fusion | bytes 458752 | tf_op jit(solution)/shard_map/gather | solution.py:163
  226.8 5.4 %copy.312 = f32[64,256,3]{1,2,0:T(4,128)S(1)} copy(f32[64,256,3]{2,1,0:T(8,128)} %bitcast.288) | data formatting | bytes 393216 | tf_op jit(solution)/shard_map/gather | solution.py:163
  233.0 30.9 %all-to-all-start = ((f32[3,64,256]{2,0,1:T(4,128)}), f32[3,64,256]{2,0,1:T(4,128)S(1)}, u32[]{:S(2)}, u32[]{:S(2)}) async-start(f32[3,64,256]{2,0,1:T(4,128)} %multiply_bitcast_fusion), calls=%async_computation | async-start | bytes 524288 | tf_op jit(solution)/shard_map/all_to_all | solution.py:164
  263.9 16.1 %fusion = f32[3,4,8,128]{3,2,1,0:T(8,128)S(1)} fusion(f32[3,4,2,8,2,128,2]{6,5,4,3,2,1,0:T(8,128)} %squeeze.11, f32[1,4,2,8,2,128,2]{6,5,4,3,2,1,0:T(8,128)} %stack.91, f32[1,4,2,8,2,128,2]{6,5,4,3,2,1,0:T(8,128)} %stack.90, f32[1,4,2,8,2,128,2]{6,5,4,3,2,1,0:T(8,128)} %stack.89), kind=kLoop, calls=%fused_computation.3 | loop fusion | flops 380928 | bytes 835584 | tf_op jit(solution)/shard_map/reduce_sum | solution.py:123
  280.7 5.1 copy.313
  285.8 88.6 %scatter_fusion = f32[3,4096]{0,1:T(8,128)S(1)} fusion(f32[3,4096]{0,1:T(8,128)S(1)} %bitcast.286, s32[16384]{0:T(1024)S(1)} %bitcast.312, f32[16384,3]{1,0:T(8,128)} %copy.313), kind=kCustom, calls=%fused_computation.1 | custom fusion | flops 49152 | bytes 655360 | tf_op jit(solution)/shard_map/scatter-add | solution.py:166
  375.3 1.3 collective-permute-start.11
  376.6 4.0 collective-permute-start.10
  382.5 1.3 collective-permute-start.13
  383.8 4.2 collective-permute-start.12
  389.6 1.3 collective-permute-start.15
  390.9 4.2 collective-permute-start.14
  396.7 1.6 copy.319
  398.4 1.6 broadcast_in_dim.34
  400.0 1.8 copy.321
  401.8 1.6 fusion.728
  404.8 1.3 collective-permute-start.17
  406.1 5.8 %collective-permute-start.16 = (f32[3,1,16,256]{3,2,1,0:T(8,128)}, f32[3,1,16,256]{3,2,1,0:T(8,128)}, u32[]{:S(2)}, u32[]{:S(2)}) collective-permute-start(f32[3,1,16,256]{3,2,1,0:T(8,128)} %get-tuple-element.52), channel_id=1, source_target_pairs={{0,4},{4,8},{8,12},{12,16},{16,20},{20,24},{24,28},{28,32},{32,36}... | collective-permute-start | bytes 147464 | tf_op jit(solution)/shard_map/ppermute | solution.py:22
  411.9 1.8 copy.320
  413.8 1.5 select_maximum_fusion
  415.5 3.3 fusion.5
  420.5 1.0 fusion.231
  421.5 1.3 copy.324
  422.9 101.1 %all-reduce.11.cloned.1.call-done = f32[8,16,256]{1,0,2:T(8,128)} async-done(((f32[8,16,256]{1,0,2:T(8,128)}), f32[8,16,256]{1,0,2:T(8,128)}) %all-reduce.11.cloned.1.call-update) | async-done | bytes 131088 | tf_op jit(solution)/shard_map/psum | solution.py:176
  524.1 1.6 constant_dynamic-slice_fusion
  (285 shorter events, 24.4 us)
Async XLA Ops:
  8.2 75.9 %copy-start.79 = (f32[16]{0:T(128)}, f32[16]{0:T(128)S(1)}, u32[]{:S(2)}) copy-start(f32[16]{0:T(128)S(1)} %broadcast_in_dim.30) | copy-start | bytes 196
  9.2 64.1 %collective-permute-start.1 = (f32[1,1,16,256]{3,2,1,0:T(8,128)S(1)}, f32[1,1,16,256]{3,2,1,0:T(8,128)S(1)}, u32[]{:S(2)}, u32[]{:S(2)}) collective-permute-start(f32[1,1,16,256]{3,2,1,0:T(8,128)S(1)} %get-tuple-element.69), channel_id=1, source_target_pairs={{4,0},{8,4},{12,8},{16,12},{20,16},{24,20},{28,24},{32,28},{36,32}... | collective-permute-start | bytes 49160 | tf_op jit(solution)/shard_map/ppermute | solution.py:25
  10.5 62.8 %collective-permute-start = (f32[1,1,16,256]{3,2,1,0:T(8,128)S(1)}, f32[1,1,16,256]{3,2,1,0:T(8,128)S(1)}, u32[]{:S(2)}, u32[]{:S(2)}) collective-permute-start(f32[1,1,16,256]{3,2,1,0:T(8,128)S(1)} %get-tuple-element.68), channel_id=1, source_target_pairs={{0,4},{4,8},{8,12},{12,16},{16,20},{20,24},{24,28},{28,32},{32,36}... | collective-permute-start | bytes 49160 | tf_op jit(solution)/shard_map/ppermute | solution.py:22
  30.4 42.7 %collective-permute-start.9 = (f32[1,1,8,128]{3,2,1,0:T(8,128)S(1)}, f32[1,1,8,128]{3,2,1,0:T(8,128)S(1)}, u32[]{:S(2)}, u32[]{:S(2)}) collective-permute-start(f32[1,1,8,128]{3,2,1,0:T(8,128)S(1)} %get-tuple-element.103), channel_id=1, source_target_pairs={{4,0},{8,4},{12,8},{16,12},{20,16},{24,20},{28,24},{32,28},{36,32}... | collective-permute-start | bytes 12296 | tf_op jit(solution)/shard_map/ppermute | solution.py:25
  31.7 41.4 %collective-permute-start.8 = (f32[1,1,8,128]{3,2,1,0:T(8,128)S(1)}, f32[1,1,8,128]{3,2,1,0:T(8,128)S(1)}, u32[]{:S(2)}, u32[]{:S(2)}) collective-permute-start(f32[1,1,8,128]{3,2,1,0:T(8,128)S(1)} %get-tuple-element.102), channel_id=1, source_target_pairs={{0,4},{4,8},{8,12},{12,16},{16,20},{20,24},{24,28},{28,32},{32,36}... | collective-permute-start | bytes 12296 | tf_op jit(solution)/shard_map/ppermute | solution.py:22
  74.0 32.9 %copy-start.15 = (f32[8,16,256]{2,1,0:T(8,128)}, f32[8,16,256]{2,1,0:T(8,128)S(1)}, u32[]{:S(2)}) copy-start(f32[8,16,256]{2,1,0:T(8,128)S(1)} %get-tuple-element.28) | copy-start | bytes 393220
  74.0 32.9 %copy-start.17 = (f32[8,16,256]{2,1,0:T(8,128)}, f32[8,16,256]{2,1,0:T(8,128)S(1)}, u32[]{:S(2)}) copy-start(f32[8,16,256]{2,1,0:T(8,128)S(1)} %get-tuple-element.29) | copy-start | bytes 393220
  74.0 32.9 %copy-start.19 = (f32[8,16,256]{2,1,0:T(8,128)}, f32[8,16,256]{2,1,0:T(8,128)S(1)}, u32[]{:S(2)}) copy-start(f32[8,16,256]{2,1,0:T(8,128)S(1)} %get-tuple-element.30) | copy-start | bytes 393220
  74.0 32.9 %copy-start.21 = (f32[8,16,256]{2,1,0:T(8,128)}, f32[8,16,256]{2,1,0:T(8,128)S(1)}, u32[]{:S(2)}) copy-start(f32[8,16,256]{2,1,0:T(8,128)S(1)} %get-tuple-element.31) | copy-start | bytes 393220
  74.0 32.9 %copy-start.23 = (f32[8,16,256]{2,1,0:T(8,128)}, f32[8,16,256]{2,1,0:T(8,128)S(1)}, u32[]{:S(2)}) copy-start(f32[8,16,256]{2,1,0:T(8,128)S(1)} %get-tuple-element.32) | copy-start | bytes 393220
  74.1 32.9 %copy-start.25 = (f32[8,16,256]{2,1,0:T(8,128)}, f32[8,16,256]{2,1,0:T(8,128)S(1)}, u32[]{:S(2)}) copy-start(f32[8,16,256]{2,1,0:T(8,128)S(1)} %get-tuple-element.33) | copy-start | bytes 393220
  74.1 32.9 %copy-start.27 = (f32[8,16,256]{2,1,0:T(8,128)}, f32[8,16,256]{2,1,0:T(8,128)S(1)}, u32[]{:S(2)}) copy-start(f32[8,16,256]{2,1,0:T(8,128)S(1)} %get-tuple-element.34) | copy-start | bytes 393220
  74.1 32.9 %copy-start.29 = (f32[8,16,256]{2,1,0:T(8,128)}, f32[8,16,256]{2,1,0:T(8,128)S(1)}, u32[]{:S(2)}) copy-start(f32[8,16,256]{2,1,0:T(8,128)S(1)} %get-tuple-element.35) | copy-start | bytes 393220
  74.1 32.9 %copy-start.31 = (f32[8,16,256]{2,1,0:T(8,128)}, f32[8,16,256]{2,1,0:T(8,128)S(1)}, u32[]{:S(2)}) copy-start(f32[8,16,256]{2,1,0:T(8,128)S(1)} %get-tuple-element.36) | copy-start | bytes 393220
  74.1 32.9 %copy-start.33 = (f32[8,16,256]{2,1,0:T(8,128)}, f32[8,16,256]{2,1,0:T(8,128)S(1)}, u32[]{:S(2)}) copy-start(f32[8,16,256]{2,1,0:T(8,128)S(1)} %get-tuple-element.37) | copy-start | bytes 393220
  74.1 32.9 %copy-start.34 = (f32[8,16,256]{2,1,0:T(8,128)}, f32[8,16,256]{2,1,0:T(8,128)S(1)}, u32[]{:S(2)}) copy-start(f32[8,16,256]{2,1,0:T(8,128)S(1)} %get-tuple-element.38) | copy-start | bytes 393220
  74.1 32.9 %copy-start.35 = (f32[8,16,256]{2,1,0:T(8,128)}, f32[8,16,256]{2,1,0:T(8,128)S(1)}, u32[]{:S(2)}) copy-start(f32[8,16,256]{2,1,0:T(8,128)S(1)} %get-tuple-element.39) | copy-start | bytes 393220
  74.1 32.9 %copy-start.36 = (f32[8,16,256]{2,1,0:T(8,128)}, f32[8,16,256]{2,1,0:T(8,128)S(1)}, u32[]{:S(2)}) copy-start(f32[8,16,256]{2,1,0:T(8,128)S(1)} %get-tuple-element.40) | copy-start | bytes 393220
  74.1 32.9 %copy-start.37 = (f32[8,16,256]{2,1,0:T(8,128)}, f32[8,16,256]{2,1,0:T(8,128)S(1)}, u32[]{:S(2)}) copy-start(f32[8,16,256]{2,1,0:T(8,128)S(1)} %get-tuple-element.41) | copy-start | bytes 393220
  74.1 32.9 %copy-start.38 = (f32[8,16,256]{2,1,0:T(8,128)}, f32[8,16,256]{2,1,0:T(8,128)S(1)}, u32[]{:S(2)}) copy-start(f32[8,16,256]{2,1,0:T(8,128)S(1)} %get-tuple-element.42) | copy-start | bytes 393220
  74.2 32.9 %copy-start.39 = (f32[8,16,256]{2,1,0:T(8,128)}, f32[8,16,256]{2,1,0:T(8,128)S(1)}, u32[]{:S(2)}) copy-start(f32[8,16,256]{2,1,0:T(8,128)S(1)} %get-tuple-element.43) | copy-start | bytes 393220
  74.2 32.9 %copy-start.40 = (f32[8,16,256]{2,1,0:T(8,128)}, f32[8,16,256]{2,1,0:T(8,128)S(1)}, u32[]{:S(2)}) copy-start(f32[8,16,256]{2,1,0:T(8,128)S(1)} %get-tuple-element.44) | copy-start | bytes 393220
  74.2 32.9 %copy-start.41 = (f32[8,16,256]{2,1,0:T(8,128)}, f32[8,16,256]{2,1,0:T(8,128)S(1)}, u32[]{:S(2)}) copy-start(f32[8,16,256]{2,1,0:T(8,128)S(1)} %get-tuple-element.45) | copy-start | bytes 393220
  74.8 22.3 %copy-start.3 = (f32[8,16,256]{2,1,0:T(8,128)}, f32[8,16,256]{2,1,0:T(8,128)S(1)}, u32[]{:S(2)}) copy-start(f32[8,16,256]{2,1,0:T(8,128)S(1)} %get-tuple-element.18) | copy-start | bytes 393220
  74.9 5.8 %collective-permute-start.3 = (f32[3,1,16,256]{3,2,1,0:T(8,128)S(1)}, f32[3,1,16,256]{3,2,1,0:T(8,128)S(1)}, u32[]{:S(2)}, u32[]{:S(2)}) collective-permute-start(f32[3,1,16,256]{3,2,1,0:T(8,128)S(1)} %get-tuple-element.59), channel_id=1, source_target_pairs={{4,0},{8,4},{12,8},{16,12},{20,16},{24,20},{28,24},{32,28},{36,32}... | collective-permute-start | bytes 147464 | tf_op jit(solution)/shard_map/ppermute | solution.py:25
  76.2 5.3 %collective-permute-start.2 = (f32[3,1,16,256]{3,2,1,0:T(8,128)S(1)}, f32[3,1,16,256]{3,2,1,0:T(8,128)S(1)}, u32[]{:S(2)}, u32[]{:S(2)}) collective-permute-start(f32[3,1,16,256]{3,2,1,0:T(8,128)S(1)} %get-tuple-element.58), channel_id=1, source_target_pairs={{0,4},{4,8},{8,12},{12,16},{16,20},{20,24},{24,28},{28,32},{32,36}... | collective-permute-start | bytes 147464 | tf_op jit(solution)/shard_map/ppermute | solution.py:22
  80.6 26.5 %copy-start.42 = (f32[8,16,256]{2,1,0:T(8,128)}, f32[8,16,256]{2,1,0:T(8,128)S(1)}, u32[]{:S(2)}) copy-start(f32[8,16,256]{2,1,0:T(8,128)S(1)} %get-tuple-element.66) | copy-start | bytes 393220
  80.6 26.5 %copy-start.43 = (f32[8,16,256]{2,1,0:T(8,128)}, f32[8,16,256]{2,1,0:T(8,128)S(1)}, u32[]{:S(2)}) copy-start(f32[8,16,256]{2,1,0:T(8,128)S(1)} %get-tuple-element.67) | copy-start | bytes 393220
  80.6 26.5 %copy-start.44 = (f32[8,16,256]{2,1,0:T(8,128)}, f32[8,16,256]{2,1,0:T(8,128)S(1)}, u32[]{:S(2)}) copy-start(f32[8,16,256]{2,1,0:T(8,128)S(1)} %get-tuple-element.104) | copy-start | bytes 393220
  80.6 26.5 %copy-start.45 = (f32[8,16,256]{2,1,0:T(8,128)}, f32[8,16,256]{2,1,0:T(8,128)S(1)}, u32[]{:S(2)}) copy-start(f32[8,16,256]{2,1,0:T(8,128)S(1)} %get-tuple-element.105) | copy-start | bytes 393220
  80.6 26.5 %copy-start.46 = (f32[8,16,256]{2,1,0:T(8,128)}, f32[8,16,256]{2,1,0:T(8,128)S(1)}, u32[]{:S(2)}) copy-start(f32[8,16,256]{2,1,0:T(8,128)S(1)} %get-tuple-element.106) | copy-start | bytes 393220
  80.6 26.5 %copy-start.47 = (f32[8,16,256]{2,1,0:T(8,128)}, f32[8,16,256]{2,1,0:T(8,128)S(1)}, u32[]{:S(2)}) copy-start(f32[8,16,256]{2,1,0:T(8,128)S(1)} %get-tuple-element.107) | copy-start | bytes 393220
  80.7 26.5 %copy-start.48 = (f32[8,16,256]{2,1,0:T(8,128)}, f32[8,16,256]{2,1,0:T(8,128)S(1)}, u32[]{:S(2)}) copy-start(f32[8,16,256]{2,1,0:T(8,128)S(1)} %get-tuple-element.108) | copy-start | bytes 393220
  80.7 26.5 %copy-start.49 = (f32[8,16,256]{2,1,0:T(8,128)}, f32[8,16,256]{2,1,0:T(8,128)S(1)}, u32[]{:S(2)}) copy-start(f32[8,16,256]{2,1,0:T(8,128)S(1)} %get-tuple-element.109) | copy-start | bytes 393220
  84.8 8.8 %collective-permute-start.5 = (f32[3,1,16,256]{3,2,1,0:T(8,128)S(1)}, f32[3,1,16,256]{3,2,1,0:T(8,128)S(1)}, u32[]{:S(2)}, u32[]{:S(2)}) collective-permute-start(f32[3,1,16,256]{3,2,1,0:T(8,128)S(1)} %get-tuple-element.57), channel_id=1, source_target_pairs={{4,0},{8,4},{12,8},{16,12},{20,16},{24,20},{28,24},{32,28},{36,32}... | collective-permute-start | bytes 147464 | tf_op jit(solution)/shard_map/ppermute | solution.py:25
  86.1 7.9 %collective-permute-start.4 = (f32[3,1,16,256]{3,2,1,0:T(8,128)S(1)}, f32[3,1,16,256]{3,2,1,0:T(8,128)S(1)}, u32[]{:S(2)}, u32[]{:S(2)}) collective-permute-start(f32[3,1,16,256]{3,2,1,0:T(8,128)S(1)} %get-tuple-element.56), channel_id=1, source_target_pairs={{0,4},{4,8},{8,12},{12,16},{16,20},{20,24},{24,28},{28,32},{32,36}... | collective-permute-start | bytes 147464 | tf_op jit(solution)/shard_map/ppermute | solution.py:22
  97.4 8.9 %collective-permute-start.7 = (f32[3,1,16,256]{3,2,1,0:T(8,128)S(1)}, f32[3,1,16,256]{3,2,1,0:T(8,128)S(1)}, u32[]{:S(2)}, u32[]{:S(2)}) collective-permute-start(f32[3,1,16,256]{3,2,1,0:T(8,128)S(1)} %get-tuple-element.55), channel_id=1, source_target_pairs={{4,0},{8,4},{12,8},{16,12},{20,16},{24,20},{28,24},{32,28},{36,32}... | collective-permute-start | bytes 147464 | tf_op jit(solution)/shard_map/ppermute | solution.py:25
  98.7 7.9 %collective-permute-start.6 = (f32[3,1,16,256]{3,2,1,0:T(8,128)S(1)}, f32[3,1,16,256]{3,2,1,0:T(8,128)S(1)}, u32[]{:S(2)}, u32[]{:S(2)}) collective-permute-start(f32[3,1,16,256]{3,2,1,0:T(8,128)S(1)} %get-tuple-element.54), channel_id=1, source_target_pairs={{0,4},{4,8},{8,12},{12,16},{16,20},{20,24},{24,28},{28,32},{32,36}... | collective-permute-start | bytes 147464 | tf_op jit(solution)/shard_map/ppermute | solution.py:22
  233.0 47.7 %all-to-all-start = ((f32[3,64,256]{2,0,1:T(4,128)}), f32[3,64,256]{2,0,1:T(4,128)S(1)}, u32[]{:S(2)}, u32[]{:S(2)}) async-start(f32[3,64,256]{2,0,1:T(4,128)} %multiply_bitcast_fusion), calls=%async_computation | async-start | bytes 524288 | tf_op jit(solution)/shard_map/all_to_all | solution.py:164
  263.9 260.2 %all-reduce.11.cloned.1.call-start = ((), (), s32[]{:S(2)}) async-start(), calls=%async_computation.1 | async-start | bytes 2097152 | tf_op jit(solution)/shard_map/psum | solution.py:176
  375.3 5.4 %collective-permute-start.11 = (f32[3,1,8,128]{3,2,1,0:T(8,128)S(1)}, f32[3,1,8,128]{3,2,1,0:T(8,128)S(1)}, u32[]{:S(2)}, u32[]{:S(2)}) collective-permute-start(f32[3,1,8,128]{3,2,1,0:T(8,128)S(1)} %get-tuple-element.99), channel_id=1, source_target_pairs={{4,0},{8,4},{12,8},{16,12},{20,16},{24,20},{28,24},{32,28},{36,32}... | collective-permute-start | bytes 36872 | tf_op jit(solution)/shard_map/ppermute | solution.py:25
  376.6 4.8 collective-permute-start.10
  382.5 5.6 %collective-permute-start.13 = (f32[3,1,8,128]{3,2,1,0:T(8,128)S(1)}, f32[3,1,8,128]{3,2,1,0:T(8,128)S(1)}, u32[]{:S(2)}, u32[]{:S(2)}) collective-permute-start(f32[3,1,8,128]{3,2,1,0:T(8,128)S(1)} %get-tuple-element.97), channel_id=1, source_target_pairs={{4,0},{8,4},{12,8},{16,12},{20,16},{24,20},{28,24},{32,28},{36,32}... | collective-permute-start | bytes 36872 | tf_op jit(solution)/shard_map/ppermute | solution.py:25
  383.8 5.1 collective-permute-start.12
  389.6 6.2 %collective-permute-start.15 = (f32[3,1,8,128]{3,2,1,0:T(8,128)S(1)}, f32[3,1,8,128]{3,2,1,0:T(8,128)S(1)}, u32[]{:S(2)}, u32[]{:S(2)}) collective-permute-start(f32[3,1,8,128]{3,2,1,0:T(8,128)S(1)} %get-tuple-element.95), channel_id=1, source_target_pairs={{4,0},{8,4},{12,8},{16,12},{20,16},{24,20},{28,24},{32,28},{36,32}... | collective-permute-start | bytes 36872 | tf_op jit(solution)/shard_map/ppermute | solution.py:25
  390.9 5.1 collective-permute-start.14
  404.8 9.0 %collective-permute-start.17 = (f32[3,1,16,256]{3,2,1,0:T(8,128)}, f32[3,1,16,256]{3,2,1,0:T(8,128)}, u32[]{:S(2)}, u32[]{:S(2)}) collective-permute-start(f32[3,1,16,256]{3,2,1,0:T(8,128)} %get-tuple-element.53), channel_id=1, source_target_pairs={{4,0},{8,4},{12,8},{16,12},{20,16},{24,20},{28,24},{32,28},{36,32}... | collective-permute-start | bytes 147464 | tf_op jit(solution)/shard_map/ppermute | solution.py:25
  406.1 7.7 %collective-permute-start.16 = (f32[3,1,16,256]{3,2,1,0:T(8,128)}, f32[3,1,16,256]{3,2,1,0:T(8,128)}, u32[]{:S(2)}, u32[]{:S(2)}) collective-permute-start(f32[3,1,16,256]{3,2,1,0:T(8,128)} %get-tuple-element.52), channel_id=1, source_target_pairs={{0,4},{4,8},{8,12},{12,16},{16,20},{20,24},{24,28},{28,32},{32,36}... | collective-permute-start | bytes 147464 | tf_op jit(solution)/shard_map/ppermute | solution.py:22
  (67 other events, 367.0 us)
Sparse Core Ops, SparseCore 0:
  423.0 101.0 all-reduce.10
where the time goes:
time: 535 us; the launch traced here: 534 us
  local copies, waits for them, and re-layouts  170 us (32%)
  other arithmetic  156 us (29%)
  waiting for transfers between devices  104 us (19%)
  starting transfers between devices  87.7 us (16%)
  between operations  16 us (3%)
    psum x1, waiting for transfers between devices, body(): total_sum = lax.psum(energy, 'load')  101 us
    scatter-add x1, other arithmetic, body(): coarse_source.reshape(3, -1).at[:, face_dst[0]].add(arrived)  88.6 us
    gather x2, local copies, waits for them, and re-layouts, body(): picked = residual.reshape(3, -1)[:, face_src[0]] * live_mask[None]  65.9 us
    ppermute x9, starting transfers between devices, extended(): lax.ppermute(lax.slice_in_dim(block, block.shape[dim] - width, None, axis...  45.2 us
    another operation x4, local copies, waits for them, and re-layouts, operate(): return jnp.stack(pieces)  37.8 us
    all_to_all x1, starting transfers between devices, body(): lax.all_to_all(picked, 'space', split_axis=1, concat_axis=1, tiled=True)  30.9 us
    squeeze x1, local copies, waits for them, and re-layouts, body(): source = load_force[0]  26.5 us
    reduce_sum x2, other arithmetic, coarsen(): grid_field.reshape(comps, size_x // 2, 2, size_y // 2, 2, size_z // 2, 2)  20.2 us
  transfers between devices with their start and end apart: 20, of which 7 were waited for; matrix products, arithmetic and copies ran while one was open for 14% of the time, Pallas kernels for 0%

commit v1 on v0

--- a/solution.py
+++ b/solution.py
@@ -173,7 +173,7 @@
     outputs = [displaced]
     rows_part = NY // lax.axis_size("load")
     start_row = lax.axis_index("load") * rows_part
-    total_sum = lax.psum(energy, "load")
+    total_sum = jnp.sum(lax.all_gather(energy, "load"), axis=0)
     energy_part = lax.dynamic_slice_in_dim(total_sum, start_row, rows_part, 1)
     own_part = lax.dynamic_slice_in_dim(own_cells, start_row, rows_part, 1)[None]
     moduli = jnp.array(MODULI, jnp.float32)[:, None, None, None]

time: 535 us -> 460 us (0.86)
  the two profiles are of different devices: /device:TPU:1 before, /device:TPU:7 now
where the time goes in v1:
time: 460 us; the launch traced here: 459 us
  local copies, waits for them, and re-layouts  166 us (36%)
  other arithmetic  156 us (34%)
  starting transfers between devices  71.6 us (16%)
  waiting for transfers between devices  41.1 us (9%)
  blocking collectives  22.1 us (5%)
    scatter-add x1, other arithmetic, body(): coarse_source.reshape(3, -1).at[:, face_dst[0]].add(arrived)  88.6 us
    gather x2, local copies, waits for them, and re-layouts, body(): picked = residual.reshape(3, -1)[:, face_src[0]] * live_mask[None]  65.6 us
    ppermute x9, starting transfers between devices, extended(): lax.ppermute(lax.slice_in_dim(block, 0, width, axis=dim), axis, backward)  42.2 us
    ppermute x9, waiting for transfers between devices, extended(): lax.ppermute(lax.slice_in_dim(block, block.shape[dim] - width, None, axis...  41.1 us
    another operation x4, local copies, waits for them, and re-layouts, operate(): return jnp.stack(pieces)  37.7 us
    squeeze x1, local copies, waits for them, and re-layouts, body(): source = load_force[0]  26.5 us
    ppermute x9, starting transfers between devices, extended(): lax.ppermute(lax.slice_in_dim(block, block.shape[dim] - width, None, axis...  24.7 us
    all_gather x1, blocking collectives, body(): total_sum = jnp.sum(lax.all_gather(energy, 'load'), axis=0)  22.1 us
  transfers between devices with their start and end apart: 19, of which 7 were waited for; matrix products, arithmetic and copies ran while one was open for 16% of the time, Pallas kernels for 0%

profile of v1, /device:TPU:7, one launch (start us, length us, event | category | flops | bytes accessed | tf_op | source)
XLA Modules:
  0.0 459.3 jit_solution(15434045661951338468)
XLA Ops:
  2.6 9.0 %collective-permute-start.1 = (f32[1,1,16,256]{3,2,1,0:T(8,128)S(1)}, f32[1,1,16,256]{3,2,1,0:T(8,128)S(1)}, u32[]{:S(2)}, u32[]{:S(2)}) collective-permute-start(f32[1,1,16,256]{3,2,1,0:T(8,128)S(1)} %get-tuple-element.69), channel_id=1, source_target_pairs={{4,0},{8,4},{12,8},{16,12},{20,16},{24,20},{28,24},{32,28},{36,32}... | collective-permute-start | bytes 49160 | tf_op jit(solution)/shard_map/ppermute | solution.py:25
  11.6 1.9 collective-permute-start
  14.6 9.8 %reshape_broadcast_in_dim.3 = f32[4,2,8,2,128,2]{5,4,3,2,1,0:T(8,128)} reshape(f32[8,16,256]{2,1,0:T(8,128)S(1)} %broadcast_multiply_fusion.1) | data formatting | bytes 262144 | tf_op jit(solution)/shard_map/reshape;broadcast_in_dim | solution.py:123
  24.3 4.1 reduce_sum.47
  28.4 8.2 %collective-permute-start.9 = (f32[1,1,8,128]{3,2,1,0:T(8,128)S(1)}, f32[1,1,8,128]{3,2,1,0:T(8,128)S(1)}, u32[]{:S(2)}, u32[]{:S(2)}) collective-permute-start(f32[1,1,8,128]{3,2,1,0:T(8,128)S(1)} %get-tuple-element.103), channel_id=1, source_target_pairs={{4,0},{8,4},{12,8},{16,12},{20,16},{24,20},{28,24},{32,28},{36,32}... | collective-permute-start | bytes 12296 | tf_op jit(solution)/shard_map/ppermute | solution.py:25
  36.6 1.9 collective-permute-start.8
  40.0 26.5 %squeeze.11 = f32[3,4,2,8,2,128,2]{6,5,4,3,2,1,0:T(8,128)} reshape(f32[1,3,8,16,256]{4,3,2,1,0:T(8,128)S(1)} %copy-done) | data formatting | bytes 786432 | tf_op jit(solution)/shard_map/squeeze | solution.py:159
  66.5 8.6 %copy.310 = f32[1,3,8,16,256]{1,4,3,2,0:T(8,128)} copy(f32[1,3,8,16,256]{4,3,2,1,0:T(8,128)S(1)} %copy-done) | data formatting | bytes 786432 | tf_op args[0]
  77.5 8.2 %collective-permute-start.3 = (f32[3,1,16,256]{3,2,1,0:T(8,128)S(1)}, f32[3,1,16,256]{3,2,1,0:T(8,128)S(1)}, u32[]{:S(2)}, u32[]{:S(2)}) collective-permute-start(f32[3,1,16,256]{3,2,1,0:T(8,128)S(1)} %get-tuple-element.59), channel_id=1, source_target_pairs={{4,0},{8,4},{12,8},{16,12},{20,16},{24,20},{28,24},{32,28},{36,32}... | collective-permute-start | bytes 147464 | tf_op jit(solution)/shard_map/ppermute | solution.py:25
  85.6 1.9 collective-permute-start.2
  87.9 7.4 %collective-permute-done.2 = f32[3,1,16,256]{3,2,1,0:T(8,128)S(1)} collective-permute-done((f32[3,1,16,256]{3,2,1,0:T(8,128)S(1)}, f32[3,1,16,256]{3,2,1,0:T(8,128)S(1)}, u32[]{:S(2)}, u32[]{:S(2)}) %collective-permute-start.2) | collective-permute-done | bytes 49184 | tf_op jit(solution)/shard_map/ppermute | solution.py:22
  95.7 2.0 fusion.164
  98.6 1.9 collective-permute-start.5
  100.5 3.4 collective-permute-start.4
  104.7 5.5 %collective-permute-done.4 = f32[3,1,16,256]{3,2,1,0:T(8,128)S(1)} collective-permute-done((f32[3,1,16,256]{3,2,1,0:T(8,128)S(1)}, f32[3,1,16,256]{3,2,1,0:T(8,128)S(1)}, u32[]{:S(2)}, u32[]{:S(2)}) %collective-permute-start.4) | collective-permute-done | bytes 49184 | tf_op jit(solution)/shard_map/ppermute | solution.py:22
  110.6 2.0 fusion.111
  113.7 1.9 collective-permute-start.7
  115.6 3.5 collective-permute-start.6
  119.9 5.3 %collective-permute-done.6 = f32[3,1,16,256]{3,2,1,0:T(8,128)S(1)} collective-permute-done((f32[3,1,16,256]{3,2,1,0:T(8,128)S(1)}, f32[3,1,16,256]{3,2,1,0:T(8,128)S(1)}, u32[]{:S(2)}, u32[]{:S(2)}) %collective-permute-start.6) | collective-permute-done | bytes 49184 | tf_op jit(solution)/shard_map/ppermute | solution.py:22
  125.9 2.0 fusion.58
  128.6 9.7 %stack.91 = f32[1,4,2,8,2,128,2]{6,5,4,3,2,1,0:T(8,128)} reshape(f32[1,8,16,256]{3,2,1,0:T(8,128)S(1)} %fusion.270) | data formatting | bytes 262144 | tf_op jit(solution)/shard_map/stack | solution.py:87
  138.3 9.7 %stack.90 = f32[1,4,2,8,2,128,2]{6,5,4,3,2,1,0:T(8,128)} reshape(f32[1,8,16,256]{3,2,1,0:T(8,128)S(1)} %get-tuple-element.23) | data formatting | bytes 262144 | tf_op jit(solution)/shard_map/stack | solution.py:87
  148.0 9.7 %stack.89 = f32[1,4,2,8,2,128,2]{6,5,4,3,2,1,0:T(8,128)} reshape(f32[1,8,16,256]{3,2,1,0:T(8,128)S(1)} %get-tuple-element.22) | data formatting | bytes 262144 | tf_op jit(solution)/shard_map/stack | solution.py:87
  158.5 8.5 %copy.311 = f32[3,32768]{0,1:T(8,128)} copy(f32[3,32768]{1,0:T(4,128)S(1)} %pad_maximum_fusion) | data formatting | bytes 786432 | tf_op jit(solution)/shard_map/stack | solution.py:87
  167.1 17.8 %bitcast_subtract_fusion = f32[3,32768]{0,1:T(8,128)} fusion(f32[3,32768]{0,1:T(8,128)} %copy.311, f32[1,3,8,16,256]{1,4,3,2,0:T(8,128)} %copy.310), kind=kLoop, calls=%fused_computation.4 | loop fusion | flops 98304 | bytes 1179648 | tf_op jit(solution)/shard_map/sub | solution.py:161
  184.9 60.2 %gather_fusion = f32[16384,3]{1,0:T(8,128)} fusion(f32[3,32768]{0,1:T(8,128)} %bitcast_subtract_fusion, s32[16384]{0:T(1024)S(1)} %copy-done.77), kind=kCustom, calls=%fused_computation | custom fusion | bytes 458752 | tf_op jit(solution)/shard_map/gather | solution.py:163
  245.1 5.4 %copy.312 = f32[64,256,3]{1,2,0:T(4,128)S(1)} copy(f32[64,256,3]{2,1,0:T(8,128)} %bitcast.289) | data formatting | bytes 393216 | tf_op jit(solution)/shard_map/gather | solution.py:163
  251.3 4.7 %all-to-all-start = ((f32[3,64,256]{2,0,1:T(4,128)}), f32[3,64,256]{2,0,1:T(4,128)S(1)}, u32[]{:S(2)}, u32[]{:S(2)}) async-start(f32[3,64,256]{2,0,1:T(4,128)} %multiply_bitcast_fusion), calls=%async_computation | async-start | bytes 524288 | tf_op jit(solution)/shard_map/all_to_all | solution.py:164
  256.0 16.1 %fusion = f32[3,4,8,128]{3,2,1,0:T(8,128)S(1)} fusion(f32[3,4,2,8,2,128,2]{6,5,4,3,2,1,0:T(8,128)} %squeeze.11, f32[1,4,2,8,2,128,2]{6,5,4,3,2,1,0:T(8,128)} %stack.91, f32[1,4,2,8,2,128,2]{6,5,4,3,2,1,0:T(8,128)} %stack.90, f32[1,4,2,8,2,128,2]{6,5,4,3,2,1,0:T(8,128)} %stack.89), kind=kLoop, calls=%fused_computation.3 | loop fusion | flops 380928 | bytes 835584 | tf_op jit(solution)/shard_map/reduce_sum | solution.py:123
  272.8 5.1 %copy.313 = f32[16384,3]{1,0:T(8,128)} copy(f32[16384,3]{0,1:T(4,128)S(1)} %bitcast.304) | data formatting | bytes 393216 | tf_op jit(solution)/shard_map/all_to_all | solution.py:164
  277.9 88.6 %scatter_fusion = f32[3,4096]{0,1:T(8,128)S(1)} fusion(f32[3,4096]{0,1:T(8,128)S(1)} %bitcast.287, s32[16384]{0:T(1024)S(1)} %bitcast.314, f32[16384,3]{1,0:T(8,128)} %copy.313), kind=kCustom, calls=%fused_computation.1 | custom fusion | flops 49152 | bytes 655360 | tf_op jit(solution)/shard_map/scatter-add | solution.py:166
  367.4 7.3 %collective-permute-start.11 = (f32[3,1,8,128]{3,2,1,0:T(8,128)S(1)}, f32[3,1,8,128]{3,2,1,0:T(8,128)S(1)}, u32[]{:S(2)}, u32[]{:S(2)}) collective-permute-start(f32[3,1,8,128]{3,2,1,0:T(8,128)S(1)} %get-tuple-element.99), channel_id=1, source_target_pairs={{4,0},{8,4},{12,8},{16,12},{20,16},{24,20},{28,24},{32,28},{36,32}... | collective-permute-start | bytes 36872 | tf_op jit(solution)/shard_map/ppermute | solution.py:25
  374.7 1.9 collective-permute-start.10
  376.7 7.2 %collective-permute-done.10 = f32[3,1,8,128]{3,2,1,0:T(8,128)S(1)} collective-permute-done((f32[3,1,8,128]{3,2,1,0:T(8,128)S(1)}, f32[3,1,8,128]{3,2,1,0:T(8,128)S(1)}, u32[]{:S(2)}, u32[]{:S(2)}) %collective-permute-start.10) | collective-permute-done | bytes 12320 | tf_op jit(solution)/shard_map/ppermute | solution.py:22
  385.0 1.9 collective-permute-start.13
  386.9 3.4 collective-permute-start.12
  390.4 5.8 %collective-permute-done.12 = f32[3,1,8,128]{3,2,1,0:T(8,128)S(1)} collective-permute-done((f32[3,1,8,128]{3,2,1,0:T(8,128)S(1)}, f32[3,1,8,128]{3,2,1,0:T(8,128)S(1)}, u32[]{:S(2)}, u32[]{:S(2)}) %collective-permute-start.12) | collective-permute-done | bytes 12320 | tf_op jit(solution)/shard_map/ppermute | solution.py:22
  396.9 1.9 collective-permute-start.15
  398.8 3.4 collective-permute-start.14
  402.8 5.3 %collective-permute-done.14 = f32[3,1,8,128]{3,2,1,0:T(8,128)S(1)} collective-permute-done((f32[3,1,8,128]{3,2,1,0:T(8,128)S(1)}, f32[3,1,8,128]{3,2,1,0:T(8,128)S(1)}, u32[]{:S(2)}, u32[]{:S(2)}) %collective-permute-start.14) | collective-permute-done | bytes 12320 | tf_op jit(solution)/shard_map/ppermute | solution.py:22
  412.2 1.8 copy.321
  414.0 1.6 fusion.728
  417.0 1.9 collective-permute-start.17
  418.9 3.4 collective-permute-start.16
  422.4 1.8 copy.320
  424.2 4.6 %collective-permute-done.16 = f32[3,1,16,256]{3,2,1,0:T(8,128)} collective-permute-done((f32[3,1,16,256]{3,2,1,0:T(8,128)}, f32[3,1,16,256]{3,2,1,0:T(8,128)}, u32[]{:S(2)}, u32[]{:S(2)}) %collective-permute-start.16) | collective-permute-done | bytes 49184 | tf_op jit(solution)/shard_map/ppermute | solution.py:22
  430.4 3.3 fusion.5
  436.4 22.1 %all-gather = f32[32,16,256]{2,1,0:T(8,128)S(1)} all-gather(f32[8,16,256]{2,1,0:T(8,128)S(1)} %get-tuple-element.12), channel_id=2, replica_groups=mesh['space'=64,'load'=4] {'load'}, dimensions={0}, use_global_device_ids=true | all-gather | bytes 655360 | tf_op jit(solution)/shard_map/all_gather | solution.py:176
  (282 shorter events, 27.6 us)
Async XLA Ops:
  1.6 96.2 %copy-start.79 = (f32[16]{0:T(128)}, f32[16]{0:T(128)S(1)}, u32[]{:S(2)}) copy-start(f32[16]{0:T(128)S(1)} %broadcast_in_dim.30) | copy-start | bytes 196
  2.6 73.2 %collective-permute-start.1 = (f32[1,1,16,256]{3,2,1,0:T(8,128)S(1)}, f32[1,1,16,256]{3,2,1,0:T(8,128)S(1)}, u32[]{:S(2)}, u32[]{:S(2)}) collective-permute-start(f32[1,1,16,256]{3,2,1,0:T(8,128)S(1)} %get-tuple-element.69), channel_id=1, source_target_pairs={{4,0},{8,4},{12,8},{16,12},{20,16},{24,20},{28,24},{32,28},{36,32}... | collective-permute-start | bytes 49160 | tf_op jit(solution)/shard_map/ppermute | solution.py:25
  11.6 64.2 %collective-permute-start = (f32[1,1,16,256]{3,2,1,0:T(8,128)S(1)}, f32[1,1,16,256]{3,2,1,0:T(8,128)S(1)}, u32[]{:S(2)}, u32[]{:S(2)}) collective-permute-start(f32[1,1,16,256]{3,2,1,0:T(8,128)S(1)} %get-tuple-element.68), channel_id=1, source_target_pairs={{0,4},{4,8},{8,12},{12,16},{16,20},{20,24},{24,28},{28,32},{32,36}... | collective-permute-start | bytes 49160 | tf_op jit(solution)/shard_map/ppermute | solution.py:22
  28.4 47.3 %collective-permute-start.9 = (f32[1,1,8,128]{3,2,1,0:T(8,128)S(1)}, f32[1,1,8,128]{3,2,1,0:T(8,128)S(1)}, u32[]{:S(2)}, u32[]{:S(2)}) collective-permute-start(f32[1,1,8,128]{3,2,1,0:T(8,128)S(1)} %get-tuple-element.103), channel_id=1, source_target_pairs={{4,0},{8,4},{12,8},{16,12},{20,16},{24,20},{28,24},{32,28},{36,32}... | collective-permute-start | bytes 12296 | tf_op jit(solution)/shard_map/ppermute | solution.py:25
  36.6 39.1 %collective-permute-start.8 = (f32[1,1,8,128]{3,2,1,0:T(8,128)S(1)}, f32[1,1,8,128]{3,2,1,0:T(8,128)S(1)}, u32[]{:S(2)}, u32[]{:S(2)}) collective-permute-start(f32[1,1,8,128]{3,2,1,0:T(8,128)S(1)} %get-tuple-element.102), channel_id=1, source_target_pairs={{0,4},{4,8},{8,12},{12,16},{16,20},{20,24},{24,28},{28,32},{32,36}... | collective-permute-start | bytes 12296 | tf_op jit(solution)/shard_map/ppermute | solution.py:22
  76.6 49.0 %copy-start.15 = (f32[8,16,256]{2,1,0:T(8,128)}, f32[8,16,256]{2,1,0:T(8,128)S(1)}, u32[]{:S(2)}) copy-start(f32[8,16,256]{2,1,0:T(8,128)S(1)} %get-tuple-element.28) | copy-start | bytes 393220
  76.6 49.0 %copy-start.17 = (f32[8,16,256]{2,1,0:T(8,128)}, f32[8,16,256]{2,1,0:T(8,128)S(1)}, u32[]{:S(2)}) copy-start(f32[8,16,256]{2,1,0:T(8,128)S(1)} %get-tuple-element.29) | copy-start | bytes 393220
  76.6 49.0 %copy-start.19 = (f32[8,16,256]{2,1,0:T(8,128)}, f32[8,16,256]{2,1,0:T(8,128)S(1)}, u32[]{:S(2)}) copy-start(f32[8,16,256]{2,1,0:T(8,128)S(1)} %get-tuple-element.30) | copy-start | bytes 393220
  76.6 49.0 %copy-start.21 = (f32[8,16,256]{2,1,0:T(8,128)}, f32[8,16,256]{2,1,0:T(8,128)S(1)}, u32[]{:S(2)}) copy-start(f32[8,16,256]{2,1,0:T(8,128)S(1)} %get-tuple-element.31) | copy-start | bytes 393220
  76.6 49.0 %copy-start.23 = (f32[8,16,256]{2,1,0:T(8,128)}, f32[8,16,256]{2,1,0:T(8,128)S(1)}, u32[]{:S(2)}) copy-start(f32[8,16,256]{2,1,0:T(8,128)S(1)} %get-tuple-element.32) | copy-start | bytes 393220
  76.7 49.0 %copy-start.25 = (f32[8,16,256]{2,1,0:T(8,128)}, f32[8,16,256]{2,1,0:T(8,128)S(1)}, u32[]{:S(2)}) copy-start(f32[8,16,256]{2,1,0:T(8,128)S(1)} %get-tuple-element.33) | copy-start | bytes 393220
  76.7 49.0 %copy-start.27 = (f32[8,16,256]{2,1,0:T(8,128)}, f32[8,16,256]{2,1,0:T(8,128)S(1)}, u32[]{:S(2)}) copy-start(f32[8,16,256]{2,1,0:T(8,128)S(1)} %get-tuple-element.34) | copy-start | bytes 393220
  76.7 49.0 %copy-start.29 = (f32[8,16,256]{2,1,0:T(8,128)}, f32[8,16,256]{2,1,0:T(8,128)S(1)}, u32[]{:S(2)}) copy-start(f32[8,16,256]{2,1,0:T(8,128)S(1)} %get-tuple-element.35) | copy-start | bytes 393220
  76.7 49.0 %copy-start.31 = (f32[8,16,256]{2,1,0:T(8,128)}, f32[8,16,256]{2,1,0:T(8,128)S(1)}, u32[]{:S(2)}) copy-start(f32[8,16,256]{2,1,0:T(8,128)S(1)} %get-tuple-element.36) | copy-start | bytes 393220
  76.7 49.0 %copy-start.33 = (f32[8,16,256]{2,1,0:T(8,128)}, f32[8,16,256]{2,1,0:T(8,128)S(1)}, u32[]{:S(2)}) copy-start(f32[8,16,256]{2,1,0:T(8,128)S(1)} %get-tuple-element.37) | copy-start | bytes 393220
  76.7 49.0 %copy-start.34 = (f32[8,16,256]{2,1,0:T(8,128)}, f32[8,16,256]{2,1,0:T(8,128)S(1)}, u32[]{:S(2)}) copy-start(f32[8,16,256]{2,1,0:T(8,128)S(1)} %get-tuple-element.38) | copy-start | bytes 393220
  76.7 49.0 %copy-start.35 = (f32[8,16,256]{2,1,0:T(8,128)}, f32[8,16,256]{2,1,0:T(8,128)S(1)}, u32[]{:S(2)}) copy-start(f32[8,16,256]{2,1,0:T(8,128)S(1)} %get-tuple-element.39) | copy-start | bytes 393220
  76.7 49.0 %copy-start.36 = (f32[8,16,256]{2,1,0:T(8,128)}, f32[8,16,256]{2,1,0:T(8,128)S(1)}, u32[]{:S(2)}) copy-start(f32[8,16,256]{2,1,0:T(8,128)S(1)} %get-tuple-element.40) | copy-start | bytes 393220
  76.7 49.0 %copy-start.37 = (f32[8,16,256]{2,1,0:T(8,128)}, f32[8,16,256]{2,1,0:T(8,128)S(1)}, u32[]{:S(2)}) copy-start(f32[8,16,256]{2,1,0:T(8,128)S(1)} %get-tuple-element.41) | copy-start | bytes 393220
  76.7 49.0 %copy-start.38 = (f32[8,16,256]{2,1,0:T(8,128)}, f32[8,16,256]{2,1,0:T(8,128)S(1)}, u32[]{:S(2)}) copy-start(f32[8,16,256]{2,1,0:T(8,128)S(1)} %get-tuple-element.42) | copy-start | bytes 393220
  76.8 49.0 %copy-start.39 = (f32[8,16,256]{2,1,0:T(8,128)}, f32[8,16,256]{2,1,0:T(8,128)S(1)}, u32[]{:S(2)}) copy-start(f32[8,16,256]{2,1,0:T(8,128)S(1)} %get-tuple-element.43) | copy-start | bytes 393220
  76.8 49.0 %copy-start.40 = (f32[8,16,256]{2,1,0:T(8,128)}, f32[8,16,256]{2,1,0:T(8,128)S(1)}, u32[]{:S(2)}) copy-start(f32[8,16,256]{2,1,0:T(8,128)S(1)} %get-tuple-element.44) | copy-start | bytes 393220
  76.8 49.0 %copy-start.41 = (f32[8,16,256]{2,1,0:T(8,128)}, f32[8,16,256]{2,1,0:T(8,128)S(1)}, u32[]{:S(2)}) copy-start(f32[8,16,256]{2,1,0:T(8,128)S(1)} %get-tuple-element.45) | copy-start | bytes 393220
  77.4 36.0 %copy-start.3 = (f32[8,16,256]{2,1,0:T(8,128)}, f32[8,16,256]{2,1,0:T(8,128)S(1)}, u32[]{:S(2)}) copy-start(f32[8,16,256]{2,1,0:T(8,128)S(1)} %get-tuple-element.18) | copy-start | bytes 393220
  77.4 36.0 %copy-start.7 = (f32[1,8,16,256]{3,2,1,0:T(8,128)}, f32[1,8,16,256]{3,2,1,0:T(8,128)S(1)}, u32[]{:S(2)}) copy-start(f32[1,8,16,256]{3,2,1,0:T(8,128)S(1)} %get-tuple-element.19) | copy-start | bytes 393220
  77.5 10.4 %collective-permute-start.3 = (f32[3,1,16,256]{3,2,1,0:T(8,128)S(1)}, f32[3,1,16,256]{3,2,1,0:T(8,128)S(1)}, u32[]{:S(2)}, u32[]{:S(2)}) collective-permute-start(f32[3,1,16,256]{3,2,1,0:T(8,128)S(1)} %get-tuple-element.59), channel_id=1, source_target_pairs={{4,0},{8,4},{12,8},{16,12},{20,16},{24,20},{28,24},{32,28},{36,32}... | collective-permute-start | bytes 147464 | tf_op jit(solution)/shard_map/ppermute | solution.py:25
  85.6 9.7 %collective-permute-start.2 = (f32[3,1,16,256]{3,2,1,0:T(8,128)S(1)}, f32[3,1,16,256]{3,2,1,0:T(8,128)S(1)}, u32[]{:S(2)}, u32[]{:S(2)}) collective-permute-start(f32[3,1,16,256]{3,2,1,0:T(8,128)S(1)} %get-tuple-element.58), channel_id=1, source_target_pairs={{0,4},{4,8},{8,12},{12,16},{16,20},{20,24},{24,28},{28,32},{32,36}... | collective-permute-start | bytes 147464 | tf_op jit(solution)/shard_map/ppermute | solution.py:22
  87.8 38.0 %copy-start.42 = (f32[8,16,256]{2,1,0:T(8,128)}, f32[8,16,256]{2,1,0:T(8,128)S(1)}, u32[]{:S(2)}) copy-start(f32[8,16,256]{2,1,0:T(8,128)S(1)} %get-tuple-element.66) | copy-start | bytes 393220
  87.8 38.0 %copy-start.43 = (f32[8,16,256]{2,1,0:T(8,128)}, f32[8,16,256]{2,1,0:T(8,128)S(1)}, u32[]{:S(2)}) copy-start(f32[8,16,256]{2,1,0:T(8,128)S(1)} %get-tuple-element.67) | copy-start | bytes 393220
  87.8 38.0 %copy-start.44 = (f32[8,16,256]{2,1,0:T(8,128)}, f32[8,16,256]{2,1,0:T(8,128)S(1)}, u32[]{:S(2)}) copy-start(f32[8,16,256]{2,1,0:T(8,128)S(1)} %get-tuple-element.104) | copy-start | bytes 393220
  87.8 38.0 %copy-start.45 = (f32[8,16,256]{2,1,0:T(8,128)}, f32[8,16,256]{2,1,0:T(8,128)S(1)}, u32[]{:S(2)}) copy-start(f32[8,16,256]{2,1,0:T(8,128)S(1)} %get-tuple-element.105) | copy-start | bytes 393220
  87.9 38.0 %copy-start.46 = (f32[8,16,256]{2,1,0:T(8,128)}, f32[8,16,256]{2,1,0:T(8,128)S(1)}, u32[]{:S(2)}) copy-start(f32[8,16,256]{2,1,0:T(8,128)S(1)} %get-tuple-element.106) | copy-start | bytes 393220
  87.9 38.0 %copy-start.47 = (f32[8,16,256]{2,1,0:T(8,128)}, f32[8,16,256]{2,1,0:T(8,128)S(1)}, u32[]{:S(2)}) copy-start(f32[8,16,256]{2,1,0:T(8,128)S(1)} %get-tuple-element.107) | copy-start | bytes 393220
  87.9 38.0 %copy-start.48 = (f32[8,16,256]{2,1,0:T(8,128)}, f32[8,16,256]{2,1,0:T(8,128)S(1)}, u32[]{:S(2)}) copy-start(f32[8,16,256]{2,1,0:T(8,128)S(1)} %get-tuple-element.108) | copy-start | bytes 393220
  87.9 38.0 %copy-start.49 = (f32[8,16,256]{2,1,0:T(8,128)}, f32[8,16,256]{2,1,0:T(8,128)S(1)}, u32[]{:S(2)}) copy-start(f32[8,16,256]{2,1,0:T(8,128)S(1)} %get-tuple-element.109) | copy-start | bytes 393220
  98.6 6.1 %collective-permute-start.5 = (f32[3,1,16,256]{3,2,1,0:T(8,128)S(1)}, f32[3,1,16,256]{3,2,1,0:T(8,128)S(1)}, u32[]{:S(2)}, u32[]{:S(2)}) collective-permute-start(f32[3,1,16,256]{3,2,1,0:T(8,128)S(1)} %get-tuple-element.57), channel_id=1, source_target_pairs={{4,0},{8,4},{12,8},{16,12},{20,16},{24,20},{28,24},{32,28},{36,32}... | collective-permute-start | bytes 147464 | tf_op jit(solution)/shard_map/ppermute | solution.py:25
  100.5 9.7 %collective-permute-start.4 = (f32[3,1,16,256]{3,2,1,0:T(8,128)S(1)}, f32[3,1,16,256]{3,2,1,0:T(8,128)S(1)}, u32[]{:S(2)}, u32[]{:S(2)}) collective-permute-start(f32[3,1,16,256]{3,2,1,0:T(8,128)S(1)} %get-tuple-element.56), channel_id=1, source_target_pairs={{0,4},{4,8},{8,12},{12,16},{16,20},{20,24},{24,28},{28,32},{32,36}... | collective-permute-start | bytes 147464 | tf_op jit(solution)/shard_map/ppermute | solution.py:22
  113.7 6.3 %collective-permute-start.7 = (f32[3,1,16,256]{3,2,1,0:T(8,128)S(1)}, f32[3,1,16,256]{3,2,1,0:T(8,128)S(1)}, u32[]{:S(2)}, u32[]{:S(2)}) collective-permute-start(f32[3,1,16,256]{3,2,1,0:T(8,128)S(1)} %get-tuple-element.55), channel_id=1, source_target_pairs={{4,0},{8,4},{12,8},{16,12},{20,16},{24,20},{28,24},{32,28},{36,32}... | collective-permute-start | bytes 147464 | tf_op jit(solution)/shard_map/ppermute | solution.py:25
  115.6 9.6 %collective-permute-start.6 = (f32[3,1,16,256]{3,2,1,0:T(8,128)S(1)}, f32[3,1,16,256]{3,2,1,0:T(8,128)S(1)}, u32[]{:S(2)}, u32[]{:S(2)}) collective-permute-start(f32[3,1,16,256]{3,2,1,0:T(8,128)S(1)} %get-tuple-element.54), channel_id=1, source_target_pairs={{0,4},{4,8},{8,12},{12,16},{16,20},{20,24},{24,28},{28,32},{32,36}... | collective-permute-start | bytes 147464 | tf_op jit(solution)/shard_map/ppermute | solution.py:22
  251.3 21.5 %all-to-all-start = ((f32[3,64,256]{2,0,1:T(4,128)}), f32[3,64,256]{2,0,1:T(4,128)S(1)}, u32[]{:S(2)}, u32[]{:S(2)}) async-start(f32[3,64,256]{2,0,1:T(4,128)} %multiply_bitcast_fusion), calls=%async_computation | async-start | bytes 524288 | tf_op jit(solution)/shard_map/all_to_all | solution.py:164
  367.4 9.3 %collective-permute-start.11 = (f32[3,1,8,128]{3,2,1,0:T(8,128)S(1)}, f32[3,1,8,128]{3,2,1,0:T(8,128)S(1)}, u32[]{:S(2)}, u32[]{:S(2)}) collective-permute-start(f32[3,1,8,128]{3,2,1,0:T(8,128)S(1)} %get-tuple-element.99), channel_id=1, source_target_pairs={{4,0},{8,4},{12,8},{16,12},{20,16},{24,20},{28,24},{32,28},{36,32}... | collective-permute-start | bytes 36872 | tf_op jit(solution)/shard_map/ppermute | solution.py:25
  374.7 9.2 %collective-permute-start.10 = (f32[3,1,8,128]{3,2,1,0:T(8,128)S(1)}, f32[3,1,8,128]{3,2,1,0:T(8,128)S(1)}, u32[]{:S(2)}, u32[]{:S(2)}) collective-permute-start(f32[3,1,8,128]{3,2,1,0:T(8,128)S(1)} %get-tuple-element.98), channel_id=1, source_target_pairs={{0,4},{4,8},{8,12},{12,16},{16,20},{20,24},{24,28},{28,32},{32,36}... | collective-permute-start | bytes 36872 | tf_op jit(solution)/shard_map/ppermute | solution.py:22
  385.0 5.4 %collective-permute-start.13 = (f32[3,1,8,128]{3,2,1,0:T(8,128)S(1)}, f32[3,1,8,128]{3,2,1,0:T(8,128)S(1)}, u32[]{:S(2)}, u32[]{:S(2)}) collective-permute-start(f32[3,1,8,128]{3,2,1,0:T(8,128)S(1)} %get-tuple-element.97), channel_id=1, source_target_pairs={{4,0},{8,4},{12,8},{16,12},{20,16},{24,20},{28,24},{32,28},{36,32}... | collective-permute-start | bytes 36872 | tf_op jit(solution)/shard_map/ppermute | solution.py:25
  386.9 9.2 %collective-permute-start.12 = (f32[3,1,8,128]{3,2,1,0:T(8,128)S(1)}, f32[3,1,8,128]{3,2,1,0:T(8,128)S(1)}, u32[]{:S(2)}, u32[]{:S(2)}) collective-permute-start(f32[3,1,8,128]{3,2,1,0:T(8,128)S(1)} %get-tuple-element.96), channel_id=1, source_target_pairs={{0,4},{4,8},{8,12},{12,16},{16,20},{20,24},{24,28},{28,32},{32,36}... | collective-permute-start | bytes 36872 | tf_op jit(solution)/shard_map/ppermute | solution.py:22
  396.9 5.9 %collective-permute-start.15 = (f32[3,1,8,128]{3,2,1,0:T(8,128)S(1)}, f32[3,1,8,128]{3,2,1,0:T(8,128)S(1)}, u32[]{:S(2)}, u32[]{:S(2)}) collective-permute-start(f32[3,1,8,128]{3,2,1,0:T(8,128)S(1)} %get-tuple-element.95), channel_id=1, source_target_pairs={{4,0},{8,4},{12,8},{16,12},{20,16},{24,20},{28,24},{32,28},{36,32}... | collective-permute-start | bytes 36872 | tf_op jit(solution)/shard_map/ppermute | solution.py:25
  398.8 9.3 %collective-permute-start.14 = (f32[3,1,8,128]{3,2,1,0:T(8,128)S(1)}, f32[3,1,8,128]{3,2,1,0:T(8,128)S(1)}, u32[]{:S(2)}, u32[]{:S(2)}) collective-permute-start(f32[3,1,8,128]{3,2,1,0:T(8,128)S(1)} %get-tuple-element.94), channel_id=1, source_target_pairs={{0,4},{4,8},{8,12},{12,16},{16,20},{20,24},{24,28},{28,32},{32,36}... | collective-permute-start | bytes 36872 | tf_op jit(solution)/shard_map/ppermute | solution.py:22
  417.0 7.3 %collective-permute-start.17 = (f32[3,1,16,256]{3,2,1,0:T(8,128)}, f32[3,1,16,256]{3,2,1,0:T(8,128)}, u32[]{:S(2)}, u32[]{:S(2)}) collective-permute-start(f32[3,1,16,256]{3,2,1,0:T(8,128)} %get-tuple-element.53), channel_id=1, source_target_pairs={{4,0},{8,4},{12,8},{16,12},{20,16},{24,20},{28,24},{32,28},{36,32}... | collective-permute-start | bytes 147464 | tf_op jit(solution)/shard_map/ppermute | solution.py:25
  418.9 10.0 %collective-permute-start.16 = (f32[3,1,16,256]{3,2,1,0:T(8,128)}, f32[3,1,16,256]{3,2,1,0:T(8,128)}, u32[]{:S(2)}, u32[]{:S(2)}) collective-permute-start(f32[3,1,16,256]{3,2,1,0:T(8,128)} %get-tuple-element.52), channel_id=1, source_target_pairs={{0,4},{4,8},{8,12},{12,16},{16,20},{20,24},{24,28},{28,32},{32,36}... | collective-permute-start | bytes 147464 | tf_op jit(solution)/shard_map/ppermute | solution.py:22
  (66 other events, 602.6 us)
